TPU v7x, 32 devices: a whole 2x2x4 slice. The times are simulated.
32 devices in a mesh: tm: 8 (over z, y), tensor: 4 (over x, core).
Axes of the slice: x: 2, y: 2, z: 4, core: 2. Of those that a mesh axis runs over, the one named last changes fastest.
Arguments:
- frames_in: bfloat16 [8, 1024, 768], P('tm'), may hold values from -16 to 16
- norm_gain: float32 [768], replicated, may hold values from 0.1 to 1.9
- w_qkv: bfloat16 [768, 3, 768], P(None, None, 'tensor'), may hold values from -0.21650635 to 0.21650635
- w_out: bfloat16 [768, 768], P('tensor'), may hold values from -0.21875 to 0.21875
- keep_runs: int32 [8, 16, 2], replicated, may hold values from 0 to 1023, as said below
- out_cotangent: bfloat16 [8, 1024, 768], P('tm'), may hold values from -6 to 6
Outputs:
- block_out: bfloat16 [8, 1024, 768], P('tm', None, 'tensor')
- grad_in: bfloat16 [8, 1024, 768], P('tm', None, 'tensor')
- grad_qkv: bfloat16 [768, 3, 768], P('tm', None, 'tensor')
- grad_proj: bfloat16 [768, 768], P('tensor', 'tm')
- grad_gain: float32 [768], P('tensor')
Inputs may be any that keep to these rules, and one draw needn't show every extreme that they name: keep_runs[t, r] = (first, length) is the r-th run of kept positions of frame t; the 16 runs of a frame are disjoint, in rising order, and lie within the frame's 1024 positions.
All inputs are finite; a program needn't handle non-finite values.
Results may differ from a plain program's by a relative error of at most 0.034.
Values may be sent and summed in bfloat16 or wider, within the bound.
No kernel may reach another device: no remote copies, remote signals or barrier semaphores. Data moves between devices by JAX's collectives and lax.ppermute only.
A program may use at most 128 MiB of HBM per device.

v0:
```python
import jax
import jax.numpy as jnp
from jax import lax
from jax.sharding import PartitionSpec as P

D = 768
H = 12
epsilon = 1e-05


def kept_table(keep_runs, first_place, place_count):
    places = first_place + jnp.arange(place_count, dtype=jnp.int32)
    starts = keep_runs[:, :, 0:1]
    lengths = keep_runs[:, :, 1:2]
    inside = (places[None, None, :] >= starts) & (places[None, None, :] < starts + lengths)
    return jnp.sum(inside.astype(jnp.int32), axis=1)


def normalize(frames_in):
    frames_float = frames_in.astype(jnp.float32)
    centre = jnp.mean(frames_float, axis=-1, keepdims=True)
    shifted = frames_float - centre
    spread = jnp.mean(shifted * shifted, axis=-1, keepdims=True)
    inverse_spread = lax.rsqrt(spread + epsilon)
    return (frames_float, shifted * inverse_spread, inverse_spread)


def attend(packed, kept_mask):
    frames, places, row_width = packed.shape
    head_width = D // H
    pieces = packed.reshape(frames, places, 3, row_width // (3 * head_width), head_width)
    scores = jnp.einsum(
        "tphd,uphd->phtu", pieces[:, :, 0], pieces[:, :, 1], preferred_element_type=jnp.float32
    )
    scores = scores * head_width ** (-0.5)
    allowed = jnp.transpose(kept_mask)[:, None, None, :] > 0
    scores = jnp.where(allowed, scores, -1000000000.0)
    row_max = jnp.max(scores, axis=-1, keepdims=True)
    exponent = jnp.exp(scores - row_max)
    weights = (exponent / jnp.sum(exponent, axis=-1, keepdims=True)).astype(jnp.bfloat16)
    mixed_rows = jnp.einsum(
        "phtu,uphd->tphd", weights, pieces[:, :, 2], preferred_element_type=jnp.float32
    )
    mixed_rows = jnp.where(kept_mask[:, :, None, None] > 0, mixed_rows, 0.0)
    return mixed_rows.astype(jnp.bfloat16).reshape(frames, places, row_width // 3)


def project(rows_in, weight):
    leading = rows_in.shape[:-1]
    flat = jnp.dot(
        rows_in.reshape(-1, rows_in.shape[-1]), weight, preferred_element_type=jnp.float32
    )
    return flat.astype(jnp.bfloat16).reshape(leading + (weight.shape[1],))


def contract_rows(left, right):
    return lax.dot_general(
        left.reshape(-1, left.shape[-1]),
        right.reshape(-1, right.shape[-1]),
        (((0,), (0,)), ((), ())),
        preferred_element_type=jnp.float32,
    )


def back_project(cotangent, weight):
    leading = cotangent.shape[:-1]
    flat = lax.dot_general(
        cotangent.reshape(-1, cotangent.shape[-1]),
        weight,
        (((1,), (1,)), ((), ())),
        preferred_element_type=jnp.float32,
    )
    return flat.reshape(leading + (weight.shape[0],))


def body(frames_in, norm_gain, w_qkv, w_out, keep_runs, out_cotangent):
    frames_here, place_total, row_width = frames_in.shape
    places_here = place_total // lax.axis_size("tm")
    width_share = row_width // lax.axis_size("tensor")
    share_start = lax.axis_index("tensor") * width_share
    channels = w_qkv.shape[2]
    w_flat = w_qkv.reshape(row_width, 3 * channels)
    kept_mask = kept_table(keep_runs, lax.axis_index("tm") * places_here, places_here)
    frames_float, standard, inverse_spread = normalize(frames_in)
    normed = (standard * norm_gain).astype(jnp.bfloat16)
    packed = project(normed, w_flat)
    packed_places = lax.all_to_all(packed, "tm", split_axis=1, concat_axis=0, tiled=True)

    def attend_here(packed_arg):
        return attend(packed_arg, kept_mask)

    mixed_places, attend_back = jax.vjp(attend_here, packed_places)
    mixed_frames = lax.all_to_all(mixed_places, "tm", split_axis=0, concat_axis=1, tiled=True)
    branch = jnp.dot(mixed_frames.reshape(-1, channels), w_out, preferred_element_type=jnp.float32)
    branch = branch.reshape(frames_here, place_total, row_width)
    branch_share = lax.psum_scatter(
        branch.astype(jnp.bfloat16), "tensor", scatter_dimension=2, tiled=True
    ).astype(jnp.float32)
    residual_share = lax.dynamic_slice_in_dim(frames_float, share_start, width_share, 2)
    block_out = (residual_share + branch_share).astype(jnp.bfloat16)
    proj_part = contract_rows(mixed_frames, out_cotangent)
    grad_proj = lax.psum_scatter(proj_part, "tm", scatter_dimension=1, tiled=True).astype(
        jnp.bfloat16
    )
    mixed_cot = back_project(out_cotangent, w_out).astype(jnp.bfloat16)
    mixed_cot_places = lax.all_to_all(mixed_cot, "tm", split_axis=1, concat_axis=0, tiled=True)
    packed_cot_places = attend_back(mixed_cot_places)[0]
    gain_share = lax.dynamic_slice_in_dim(norm_gain, share_start, width_share, 0)
    standard_share = lax.dynamic_slice_in_dim(standard, share_start, width_share, 2)
    packed_cot = lax.all_to_all(packed_cot_places, "tm", split_axis=0, concat_axis=1, tiled=True)
    qkv_part = contract_rows(normed, packed_cot)
    normed_part = back_project(packed_cot, w_flat)
    whole_cot = lax.psum(normed_part.astype(jnp.bfloat16), "tensor").astype(jnp.float32)
    whole_cot = lax.optimization_barrier(whole_cot.astype(jnp.bfloat16)).astype(jnp.float32)
    scaled_whole = whole_cot * norm_gain
    mean_plain = jnp.mean(scaled_whole, axis=-1, keepdims=True)
    mean_cross = jnp.mean(scaled_whole * standard, axis=-1, keepdims=True)
    cot_share = lax.dynamic_slice_in_dim(whole_cot, share_start, width_share, 2)
    scaled_share = cot_share * gain_share
    through = inverse_spread * (scaled_share - mean_plain - standard_share * mean_cross)
    gain_part = jnp.sum(cot_share * standard_share, axis=(0, 1))
    cot_share_out = lax.dynamic_slice_in_dim(out_cotangent, share_start, width_share, 2).astype(
        jnp.float32
    )
    grad_in = (cot_share_out + through).astype(jnp.bfloat16)
    grad_qkv = lax.psum_scatter(
        qkv_part.reshape(row_width, 3, channels), "tm", scatter_dimension=0, tiled=True
    ).astype(jnp.bfloat16)
    grad_gain = lax.psum(gain_part, "tm")
    return (block_out, grad_in, grad_qkv, grad_proj, grad_gain)


def solution(mesh):
    in_specs = (
        P("tm", None, None),
        P(),
        P(None, None, "tensor"),
        P("tensor", None),
        P(),
        P("tm", None, None),
    )
    out_specs = (
        P("tm", None, "tensor"),
        P("tm", None, "tensor"),
        P("tm", None, "tensor"),
        P("tensor", "tm"),
        P("tensor"),
    )
    return jax.shard_map(body, mesh=mesh, in_specs=in_specs, out_specs=out_specs, check_vma=False)
```

profile of v0, /device:TPU:0, one launch (start us, length us, event | category | flops | bytes accessed | tf_op | source)
XLA Modules:
  0.0 338.7 jit_solution(6467486779215469923)
XLA Ops:
  8.0 2.2 fusion.29
  10.2 0.8 copy.115
  11.0 0.5 broadcast.97
  11.6 4.9 %reduce.4 = bf16[1024,192]{1,0:T(8,128)(2,1)} reduce(bf16[1024,1,192]{2,1,0:T(2,128)(2,1)S(1)} %bitcast.147, bf16[]{:T(256)} %broadcast.97), dimensions={1}, to_apply=%bitcast.110.reduce_sub_computation | reduce | bytes 786434
  16.5 2.4 reshape.160
  18.9 7.7 %all-to-all-start.2 = ((bf16[8,2,12288]{2,1,0:T(2,128)(2,1)}), bf16[8,2,12288]{2,1,0:T(2,128)(2,1)S(1)}, u32[]{:S(2)}, u32[]{:S(2)}) async-start(bf16[8,2,12288]{2,1,0:T(2,128)(2,1)} %reshape.160), calls=%async_computation.2 | async-start | bytes 786432 | tf_op jit(solution)/shard_map/all_to_all | solution.py:106
  27.0 0.6 multiply_reduce_fusion.1
  27.6 2.3 fusion.17
  29.9 6.2 %copy.106 = bf16[1,1024,576]{2,0,1:T(2,128)(2,1)} copy(bf16[1,1024,576]{1,2,0:T(8,128)(2,1)} %fusion.17) | data formatting | bytes 2359296 | tf_op jit(solution)/shard_map/reshape | solution.py:53
  36.1 11.0 %reduce.5 = bf16[1024,576]{1,0:T(8,128)(2,1)} reduce(bf16[1024,1,576]{2,1,0:T(2,128)(2,1)} %bitcast.141, bf16[]{:T(256)} %broadcast.97), dimensions={1}, to_apply=%bitcast.108.reduce_sub_computation | reduce | bytes 2359298
  47.1 4.4 %reshape.158 = bf16[8,2,36864]{2,1,0:T(2,128)(2,1)} reshape(bf16[1024,576]{1,0:T(8,128)(2,1)} %reduce.5) | data formatting | bytes 2359296
  51.5 17.1 %all-to-all-start = ((bf16[8,2,36864]{2,1,0:T(2,128)(2,1)}), bf16[8,2,36864]{2,1,0:T(2,128)(2,1)}, u32[]{:S(2)}, u32[]{:S(2)}) async-start(bf16[8,2,36864]{2,1,0:T(2,128)(2,1)} %reshape.158), calls=%async_computation | async-start | bytes 2359296 | tf_op jit(solution)/shard_map/all_to_all | solution.py:87
  69.0 2.4 reshape.161
  71.4 1.7 copy.116
  73.1 1.8 copy.143
  74.9 22.0 %all-to-all-done = bf16[8,2,36864]{2,1,0:T(2,128)(2,1)} async-done(((bf16[8,2,36864]{2,1,0:T(2,128)(2,1)}), bf16[8,2,36864]{2,1,0:T(2,128)(2,1)}, u32[]{:S(2)}, u32[]{:S(2)}) %all-to-all-start) | async-done | bytes 1179680 | tf_op jit(solution)/shard_map/all_to_all | solution.py:87
  96.9 6.5 %reshape.159 = bf16[1024,1,576]{2,1,0:T(2,128)(2,1)} reshape(bf16[8,2,36864]{2,1,0:T(2,128)(2,1)} %all-to-all-done) | data formatting | bytes 2359296
  103.4 6.0 %copy.107 = bf16[1,1024,576]{1,2,0:T(8,128)(2,1)} copy(bf16[1,1024,576]{2,0,1:T(2,128)(2,1)} %bitcast.142) | data formatting | bytes 2359296 | tf_op jit(solution)/shard_map/all_to_all | solution.py:87
  109.4 1.6 copy.142
  111.0 1.0 fusion.60
  112.0 1.6 copy.138
  113.6 2.7 copy.137
  116.3 2.4 copy.139
  118.7 2.0 fusion.62
  120.8 0.7 fusion.32
  121.5 0.8 multiply_divide_fusion
  122.5 1.6 fusion.39
  124.0 2.3 copy.113
  126.3 2.1 fusion.41
  128.4 3.5 %all-to-all-start.1 = ((bf16[8,128,192]{1,2,0:T(8,128)(2,1)}), bf16[8,128,192]{1,2,0:T(8,128)(2,1)S(1)}, u32[]{:S(2)}, u32[]{:S(2)}) async-start(bf16[8,128,192]{1,2,0:T(8,128)(2,1)} %bitcast.149), calls=%async_computation.1 | async-start | bytes 786432 | tf_op jit(solution)/shard_map/all_to_all | solution.py:93
  131.9 2.2 copy.118
  134.1 3.7 %convert_reduce_fusion.1 = (f32[128,3,8]{2,1,0:T(4,128)S(1)}, pred[128,3,8,8]{2,3,1,0:T(8,128)(4,1)S(1)}, f32[128,3,8]{2,1,0:T(4,128)S(1)}, bf16[128,3,8,8]{2,3,1,0:T(8,128)(2,1)S(1)}) fusion(f32[128,3,8,8]{2,3,1,0:T(8,128)} %copy-done.2, f32[128,3,8]{2,1,0:T(4,128)S(1)} %get-tuple-element.57, f32[128,3,8]{2,1,0:T(4,128)} %multiply_divide_fusion, ...), kind=kOutput, calls=%fused_computation.25 | convolution fusion | flops 3336192 | bytes 1007616 | tf_op jit(solution)/shard_map/transpose(jvp(phtu,uphd->tphd))/dot_general | solution.py:41
  137.9 1.0 fusion.58
  139.0 1.0 fusion.22
  140.2 0.7 fusion.21
  140.8 0.5 copy-done.12
  141.3 0.6 fusion.20
  141.9 2.0 pad_add_fusion
  143.9 4.0 %copy.121 = bf16[8,128,3,3,64]{1,4,3,2,0:T(8,128)(2,1)} copy(bf16[8,128,3,3,64]{4,0,3,1,2:T(8,128)(2,1)} %pad_add_fusion) | data formatting | bytes 2359296 | tf_op jit(solution)/shard_map/transpose(jvp())/add_any | solution.py:33
  147.9 6.0 %all-to-all-start.3 = ((bf16[8,128,576]{1,2,0:T(8,128)(2,1)}), bf16[8,128,576]{1,2,0:T(8,128)(2,1)}, u32[]{:S(2)}, u32[]{:S(2)}) async-start(bf16[8,128,576]{1,2,0:T(8,128)(2,1)} %bitcast.144), calls=%async_computation.3 | async-start | bytes 2359296 | tf_op jit(solution)/shard_map/all_to_all | solution.py:110
  153.9 3.0 fusion.23
  157.0 28.6 %all-to-all-done.3 = bf16[8,128,576]{1,2,0:T(8,128)(2,1)} async-done(((bf16[8,128,576]{1,2,0:T(8,128)(2,1)}), bf16[8,128,576]{1,2,0:T(8,128)(2,1)}, u32[]{:S(2)}, u32[]{:S(2)}) %all-to-all-start.3) | async-done | bytes 1179680 | tf_op jit(solution)/shard_map/all_to_all | solution.py:110
  185.6 3.9 %fusion.16 = bf16[1,1024,768]{2,1,0:T(8,128)(2,1)} fusion(bf16[768,576]{0,1:T(8,128)(2,1)S(1)} %bitcast.139, bf16[8,128,576]{1,2,0:T(8,128)(2,1)} %all-to-all-done.3), kind=kOutput, calls=%fused_computation.31 | convolution fusion | flops 906756096 | bytes 3637248 | tf_op jit(solution)/shard_map/dot_general | solution.py:67
  189.6 0.9 copy-done.10
  190.5 1.8 fusion.15
  192.2 8.5 %copy.130 = bf16[1,1024,768]{1,0,2:T(2,128)(2,1)} copy(bf16[1,1024,768]{2,1,0:T(8,128)(2,1)} %fusion.15) | data formatting | bytes 3145728
  200.7 3.7 %copy.158 = bf16[768,1,1024]{2,0,1:T(8,128)(2,1)} copy(bf16[768,1,1024]{2,1,0:T(2,128)(2,1)} %bitcast.140) | data formatting | bytes 3145728
  204.7 1.4 copy_bitcast_fusion.1
  206.1 3.3 fusion.4
  209.4 1.9 convert_element_type.92
  211.4 15.4 %reduce-scatter.12.cloned.1.call-done = f32[96,192]{1,0:T(8,128)} async-done(((f32[768,192]{1,0:T(8,128)}), f32[96,192]{1,0:T(8,128)}) %reduce-scatter.12.cloned.1.call-update) | async-done | bytes 73744
  226.8 1.6 copy.133
  228.4 3.5 %all-reduce.5.cloned.1.call-done = bf16[1,1024,768]{2,1,0:T(8,128)(2,1)} async-done(((bf16[1,1024,768]{2,1,0:T(8,128)(2,1)}), bf16[1,1024,768]{2,1,0:T(8,128)(2,1)}) %all-reduce.5.cloned.1.call-update) | async-done | bytes 1572880 | tf_op jit(solution)/shard_map/psum | solution.py:113
  232.0 1.8 convert_element_type.118
  233.9 1.2 multiply_reduce_fusion.2
  235.1 2.5 multiply_reduce_fusion.3
  237.6 0.9 copy.125
  238.5 21.8 %psum.15 = f32[192]{0:T(256)} all-reduce(f32[192]{0:T(256)S(1)} %get-tuple-element.46), channel_id=1, replica_groups=mesh['tm'=8,'tensor'=4] {'tm'}, use_global_device_ids=true, to_apply=%region_15.16 | all-reduce | flops 192 | bytes 1536 | tf_op jit(solution)/shard_map/psum | solution.py:129
  260.4 1.4 reshape_bitcast_fusion
  261.8 1.1 copy.131
  262.9 1.8 add_convert_fusion.1
  264.7 0.9 copy.124
  265.6 64.1 %reduce-scatter.8.cloned.1.call-done = f32[96,3,192]{2,0,1:T(8,128)} async-done(((f32[768,3,192]{2,0,1:T(8,128)}), f32[96,3,192]{2,0,1:T(8,128)}) %reduce-scatter.8.cloned.1.call-update) | async-done | bytes 221200 | tf_op jit(solution)/shard_map/reduce_scatter | solution.py:126
  329.7 1.6 convert_element_type.120
  (53 shorter events, 1.8 us)
Async XLA Ops:
  8.0 19.6 %copy-start = (bf16[768,3,192]{0,2,1:T(8,128)(2,1)S(1)}, bf16[768,3,192]{0,2,1:T(8,128)(2,1)}, u32[]{:S(2)}) copy-start(bf16[768,3,192]{0,2,1:T(8,128)(2,1)} %param.8) | copy-start | bytes 2654212
  11.6 15.1 %copy-start.1 = (bf16[1,1024,768]{2,1,0:T(8,128)(2,1)S(1)}, bf16[1,1024,768]{2,1,0:T(8,128)(2,1)}, u32[]{:S(2)}) copy-start(bf16[1,1024,768]{2,1,0:T(8,128)(2,1)} %param.6) | copy-start | bytes 4718596
  18.9 32.6 %all-to-all-start.2 = ((bf16[8,2,12288]{2,1,0:T(2,128)(2,1)}), bf16[8,2,12288]{2,1,0:T(2,128)(2,1)S(1)}, u32[]{:S(2)}, u32[]{:S(2)}) async-start(bf16[8,2,12288]{2,1,0:T(2,128)(2,1)} %reshape.160), calls=%async_computation.2 | async-start | bytes 786432 | tf_op jit(solution)/shard_map/all_to_all | solution.py:106
  26.7 0.9 copy-start.14
  51.5 17.2 %copy-start.13 = (s32[8,16,2]{1,2,0:T(2,128)S(1)}, s32[8,16,2]{1,2,0:T(2,128)}, u32[]{:S(2)}) copy-start(s32[8,16,2]{1,2,0:T(2,128)} %param.10) | copy-start | bytes 3076
  51.5 17.5 %copy-start.8 = (bf16[8,2,12288]{2,1,0:T(2,128)(2,1)}, bf16[8,2,12288]{2,1,0:T(2,128)(2,1)S(1)}, u32[]{:S(2)}) copy-start(bf16[8,2,12288]{2,1,0:T(2,128)(2,1)S(1)} %all-to-all-done.2) | copy-start | bytes 1179652
  51.5 45.4 %all-to-all-start = ((bf16[8,2,36864]{2,1,0:T(2,128)(2,1)}), bf16[8,2,36864]{2,1,0:T(2,128)(2,1)}, u32[]{:S(2)}, u32[]{:S(2)}) async-start(bf16[8,2,36864]{2,1,0:T(2,128)(2,1)} %reshape.158), calls=%async_computation | async-start | bytes 2359296 | tf_op jit(solution)/shard_map/all_to_all | solution.py:87
  113.6 7.1 %copy-start.5 = (bf16[8,128,1,3,64]{4,0,3,1,2:T(8,128)(2,1)}, bf16[8,128,1,3,64]{4,0,3,1,2:T(8,128)(2,1)S(1)}, u32[]{:S(2)}) copy-start(bf16[8,128,1,3,64]{4,0,3,1,2:T(8,128)(2,1)S(1)} %copy.138) | copy-start | bytes 1179652
  120.7 1.5 copy-start.2
  120.7 1.7 copy-start.11
  122.4 3.9 %copy-start.9 = (bf16[24,8,8,128]{3,2,1,0:T(8,128)(2,1)S(1)}, bf16[24,8,8,128]{3,2,1,0:T(8,128)(2,1)}, u32[]{:S(2)}) copy-start(bf16[24,8,8,128]{3,2,1,0:T(8,128)(2,1)} %copy.143) | copy-start | bytes 1179652
  128.4 19.5 %all-to-all-start.1 = ((bf16[8,128,192]{1,2,0:T(8,128)(2,1)}), bf16[8,128,192]{1,2,0:T(8,128)(2,1)S(1)}, u32[]{:S(2)}, u32[]{:S(2)}) async-start(bf16[8,128,192]{1,2,0:T(8,128)(2,1)} %bitcast.149), calls=%async_computation.1 | async-start | bytes 786432 | tf_op jit(solution)/shard_map/all_to_all | solution.py:93
  134.1 3.8 %copy-start.3 = (f32[128,3,8,8]{2,3,1,0:T(8,128)S(1)}, f32[128,3,8,8]{2,3,1,0:T(8,128)}, u32[]{:S(2)}) copy-start(f32[128,3,8,8]{2,3,1,0:T(8,128)} %copy-done.2) | copy-start | bytes 294916
  137.9 1.1 copy-start.7
  139.0 1.1 copy-start.6
  140.2 1.1 copy-start.12
  147.9 37.7 %all-to-all-start.3 = ((bf16[8,128,576]{1,2,0:T(8,128)(2,1)}), bf16[8,128,576]{1,2,0:T(8,128)(2,1)}, u32[]{:S(2)}, u32[]{:S(2)}) async-start(bf16[8,128,576]{1,2,0:T(8,128)(2,1)} %bitcast.144), calls=%async_computation.3 | async-start | bytes 2359296 | tf_op jit(solution)/shard_map/all_to_all | solution.py:110
  153.9 72.9 %reduce-scatter.12.cloned.1.call-start = ((), (), s32[]{:S(2)}) async-start(), calls=%async_computation.10 | async-start | bytes 884736
  157.0 75.0 %all-reduce.5.cloned.1.call-start = ((), (), s32[]{:S(2)}) async-start(), calls=%async_computation.7 | async-start | bytes 3145728 | tf_op jit(solution)/shard_map/psum | solution.py:113
  189.5 1.0 copy-start.10
  189.5 70.8 %reduce-scatter.10.cloned.1.call-start = ((), (), s32[]{:S(2)}) async-start(), calls=%async_computation.9 | async-start | bytes 1966080
  204.4 125.2 %reduce-scatter.8.cloned.1.call-start = ((), (), s32[]{:S(2)}) async-start(), calls=%async_computation.8 | async-start | bytes 2654208 | tf_op jit(solution)/shard_map/reduce_scatter | solution.py:126
  232.0 2.0 copy-start.4
Sparse Core Ops, SparseCore 0:
  158.0 68.7 reduce-scatter.11
  229.4 27.0 reduce-scatter.9
  260.0 69.6 reduce-scatter.7
Sparse Core Ops, SparseCore 1:
  189.6 42.3 all-reduce.4
where the time goes:
time: 345 us; the launch traced here: 339 us
  waiting for transfers between devices  134 us (39%)
  local copies, waits for them, and re-layouts  72.4 us (21%)
  starting transfers between devices  34.6 us (10%)
  other arithmetic  34.4 us (10%)
  matrix products  25.9 us (8%)
  blocking collectives  21.8 us (6%)
  between operations  15.8 us (5%)
    reduce_scatter x1, waiting for transfers between devices, body(): lax.psum_scatter(qkv_part.reshape(row_width, 3, channels), 'tm', scatter_...  64.1 us
    unnamed x47, local copies, waits for them, and re-layouts  46.5 us
    all_to_all x1, waiting for transfers between devices, body(): lax.all_to_all(packed_cot_places, 'tm', split_axis=0, concat_axis=1, tile...  28.6 us
    all_to_all x1, waiting for transfers between devices, body(): lax.all_to_all(packed, 'tm', split_axis=1, concat_axis=0, tiled=True)  22 us
    psum x1, blocking collectives, body(): grad_gain = lax.psum(gain_part, 'tm')  21.8 us
    all_to_all x1, starting transfers between devices, body(): lax.all_to_all(packed, 'tm', split_axis=1, concat_axis=0, tiled=True)  17.1 us
    unnamed x2, other arithmetic  16 us
    unnamed x6, waiting for transfers between devices  15.5 us
  transfers between devices with their start and end apart: 8, of which 5 were waited for; matrix products, arithmetic and copies ran while one was open for 26% of the time, Pallas kernels for 0%

commit v1 on v0

--- a/solution.py
+++ b/solution.py
@@ -126,7 +126,11 @@
     grad_qkv = lax.psum_scatter(
         qkv_part.reshape(row_width, 3, channels), "tm", scatter_dimension=0, tiled=True
     ).astype(jnp.bfloat16)
-    grad_gain = lax.psum(gain_part, "tm")
+    grad_gain = gain_part
+    for hop in (1, 2, 4):
+        grad_gain = grad_gain + lax.ppermute(
+            grad_gain, "tm", [(dev, dev ^ hop) for dev in range(8)]
+        )
     return (block_out, grad_in, grad_qkv, grad_proj, grad_gain)
 
 

time: 345 us -> 364 us (1.055)
  waiting for transfers between devices: 134 us -> 154 us
  starting transfers between devices: 34.6 us -> 23.1 us
  blocking collectives: 21.8 us -> 32.7 us
    all_to_all x0 -> x1, blocking collectives: none -> 32.7 us  [body(): lax.all_to_all(packed_cot_places, 'tm', split_axis=0, concat_axis=1, tile...]
    all_to_all x1 -> x0, waiting for transfers between devices: 28.6 us -> none  [body(): lax.all_to_all(packed_cot_places, 'tm', split_axis=0, concat_axis=1, tile...]
    unnamed x6, waiting for transfers between devices: 15.5 us -> 37.7 us
    psum x1 -> x0, blocking collectives: 21.8 us -> none  [body(): grad_gain = lax.psum(gain_part, 'tm')]
    psum x1, waiting for transfers between devices: 3.54 us -> 15.2 us  [body(): lax.psum(normed_part.astype(jnp.bfloat16), 'tensor').astype(jnp.float32)]
    all_to_all x1, starting transfers between devices: 17.1 us -> 6.23 us  [body(): lax.all_to_all(packed, 'tm', split_axis=1, concat_axis=0, tiled=True)]
    all_to_all x1, waiting for transfers between devices: 0.01 us -> 7.05 us  [body(): lax.all_to_all(mixed_places, 'tm', split_axis=0, concat_axis=1, tiled=True)]
    all_to_all x1 -> x0, starting transfers between devices: 5.97 us -> none  [body(): lax.all_to_all(packed_cot_places, 'tm', split_axis=0, concat_axis=1, tile...]
  transfers between devices with their start and end apart: 8 -> 10, of which waited for: 5 -> 8; matrix products, arithmetic and copies ran while one was open for 26% -> 20% of each run, Pallas kernels for 0% -> 0%
where the time goes in v1:
time: 364 us; the launch traced here: 358 us
  waiting for transfers between devices  154 us (42%)
  local copies, waits for them, and re-layouts  71.2 us (20%)
  other arithmetic  34.9 us (10%)
  blocking collectives  32.7 us (9%)
  matrix products  25.9 us (7%)
  starting transfers between devices  23.1 us (6%)
  between operations  16.3 us (4%)
    reduce_scatter x1, waiting for transfers between devices, body(): lax.psum_scatter(qkv_part.reshape(row_width, 3, channels), 'tm', scatter_...  67.9 us
    unnamed x49, local copies, waits for them, and re-layouts  45 us
    unnamed x6, waiting for transfers between devices  37.7 us
    all_to_all x1, blocking collectives, body(): lax.all_to_all(packed_cot_places, 'tm', split_axis=0, concat_axis=1, tile...  32.7 us
    all_to_all x1, waiting for transfers between devices, body(): lax.all_to_all(packed, 'tm', split_axis=1, concat_axis=0, tiled=True)  22 us
    unnamed x2, other arithmetic  16 us
    psum x1, waiting for transfers between devices, body(): lax.psum(normed_part.astype(jnp.bfloat16), 'tensor').astype(jnp.float32)  15.2 us
    all_to_all x1, starting transfers between devices, body(): lax.all_to_all(mixed_cot, 'tm', split_axis=1, concat_axis=0, tiled=True)  7.8 us
  transfers between devices with their start and end apart: 10, of which 8 were waited for; matrix products, arithmetic and copies ran while one was open for 20% of the time, Pallas kernels for 0%

profile of v1, /device:TPU:0, one launch (start us, length us, event | category | flops | bytes accessed | tf_op | source)
XLA Modules:
  0.0 358.1 jit_solution(14929947686857915444)
XLA Ops:
  8.0 2.2 fusion.29
  10.2 0.8 copy.115
  11.6 4.9 %reduce.4 = bf16[1024,192]{1,0:T(8,128)(2,1)} reduce(bf16[1024,1,192]{2,1,0:T(2,128)(2,1)S(1)} %bitcast.147, bf16[]{:T(256)} %broadcast.97), dimensions={1}, to_apply=%bitcast.110.reduce_sub_computation | reduce | bytes 786434
  16.5 2.4 reshape.160
  18.9 7.8 %all-to-all-start.2 = ((bf16[8,2,12288]{2,1,0:T(2,128)(2,1)}), bf16[8,2,12288]{2,1,0:T(2,128)(2,1)S(1)}, u32[]{:S(2)}, u32[]{:S(2)}) async-start(bf16[8,2,12288]{2,1,0:T(2,128)(2,1)} %reshape.160), calls=%async_computation.2 | async-start | bytes 786432 | tf_op jit(solution)/shard_map/all_to_all | solution.py:106
  27.7 2.3 fusion.17
  30.0 6.2 %copy.106 = bf16[1,1024,576]{2,0,1:T(2,128)(2,1)} copy(bf16[1,1024,576]{1,2,0:T(8,128)(2,1)} %fusion.17) | data formatting | bytes 2359296 | tf_op jit(solution)/shard_map/reshape | solution.py:53
  36.2 11.0 %reduce.5 = bf16[1024,576]{1,0:T(8,128)(2,1)} reduce(bf16[1024,1,576]{2,1,0:T(2,128)(2,1)} %bitcast.141, bf16[]{:T(256)} %broadcast.97), dimensions={1}, to_apply=%bitcast.108.reduce_sub_computation | reduce | bytes 2359298
  47.2 4.4 %reshape.158 = bf16[8,2,36864]{2,1,0:T(2,128)(2,1)} reshape(bf16[1024,576]{1,0:T(8,128)(2,1)} %reduce.5) | data formatting | bytes 2359296
  51.6 6.2 %all-to-all-start = ((bf16[8,2,36864]{2,1,0:T(2,128)(2,1)}), bf16[8,2,36864]{2,1,0:T(2,128)(2,1)}, u32[]{:S(2)}, u32[]{:S(2)}) async-start(bf16[8,2,36864]{2,1,0:T(2,128)(2,1)} %reshape.158), calls=%async_computation | async-start | bytes 2359296 | tf_op jit(solution)/shard_map/all_to_all | solution.py:87
  58.2 2.4 reshape.161
  60.6 1.7 copy.116
  62.3 1.8 copy.143
  64.1 22.0 %all-to-all-done = bf16[8,2,36864]{2,1,0:T(2,128)(2,1)} async-done(((bf16[8,2,36864]{2,1,0:T(2,128)(2,1)}), bf16[8,2,36864]{2,1,0:T(2,128)(2,1)}, u32[]{:S(2)}, u32[]{:S(2)}) %all-to-all-start) | async-done | bytes 1179680 | tf_op jit(solution)/shard_map/all_to_all | solution.py:87
  86.1 6.5 %reshape.159 = bf16[1024,1,576]{2,1,0:T(2,128)(2,1)} reshape(bf16[8,2,36864]{2,1,0:T(2,128)(2,1)} %all-to-all-done) | data formatting | bytes 2359296
  92.6 6.0 %copy.107 = bf16[1,1024,576]{1,2,0:T(8,128)(2,1)} copy(bf16[1,1024,576]{2,0,1:T(2,128)(2,1)} %bitcast.142) | data formatting | bytes 2359296 | tf_op jit(solution)/shard_map/all_to_all | solution.py:87
  98.6 1.6 copy.142
  100.2 1.0 fusion.60
  101.2 1.6 copy.138
  102.8 2.5 copy.137
  105.3 2.4 copy.139
  107.7 2.0 fusion.62
  109.7 0.7 fusion.32
  110.4 0.8 multiply_divide_fusion
  111.4 1.6 fusion.39
  113.0 2.3 copy.113
  115.3 2.2 fusion.41
  117.5 2.2 copy.118
  119.8 2.4 fusion.20
  122.5 1.9 convert_reduce_fusion.1
  124.5 1.0 fusion.58
  125.6 1.0 fusion.22
  127.2 2.0 pad_add_fusion
  129.2 4.2 %copy.121 = bf16[8,128,3,3,64]{1,4,3,2,0:T(8,128)(2,1)} copy(bf16[8,128,3,3,64]{4,0,3,1,2:T(8,128)(2,1)} %pad_add_fusion) | data formatting | bytes 2359296 | tf_op jit(solution)/shard_map/transpose(jvp())/add_any | solution.py:33
  133.4 32.7 %all_to_all.16 = bf16[8,128,576]{1,2,0:T(8,128)(2,1)} all-to-all(bf16[8,128,576]{1,2,0:T(8,128)(2,1)} %bitcast.144), channel_id=1, replica_groups=mesh['tm'=8,'tensor'=4] {'tm'}, dimensions={0} | all-to-all | bytes 2359296 | tf_op jit(solution)/shard_map/all_to_all | solution.py:110
  166.1 3.5 all-to-all-start.1
  169.6 3.8 %fusion.16 = bf16[1,1024,768]{2,1,0:T(8,128)(2,1)} fusion(bf16[768,576]{0,1:T(8,128)(2,1)S(1)} %bitcast.139, bf16[8,128,576]{1,2,0:T(8,128)(2,1)} %all_to_all.16), kind=kOutput, calls=%fused_computation.31 | convolution fusion | flops 906756096 | bytes 3637248 | tf_op jit(solution)/shard_map/dot_general | solution.py:67
  173.5 7.0 %all-to-all-done.1 = bf16[8,128,192]{1,2,0:T(8,128)(2,1)S(1)} async-done(((bf16[8,128,192]{1,2,0:T(8,128)(2,1)}), bf16[8,128,192]{1,2,0:T(8,128)(2,1)S(1)}, u32[]{:S(2)}, u32[]{:S(2)}) %all-to-all-start.1) | async-done | bytes 393248 | tf_op jit(solution)/shard_map/all_to_all | solution.py:93
  180.6 3.0 fusion.23
  183.7 1.8 fusion.15
  185.5 8.4 %copy.130 = bf16[1,1024,768]{1,0,2:T(2,128)(2,1)} copy(bf16[1,1024,768]{2,1,0:T(8,128)(2,1)} %fusion.15) | data formatting | bytes 3145728
  193.9 3.7 %copy.158 = bf16[768,1,1024]{2,0,1:T(8,128)(2,1)} copy(bf16[768,1,1024]{2,1,0:T(2,128)(2,1)} %bitcast.140) | data formatting | bytes 3145728
  197.7 1.4 copy_bitcast_fusion.1
  199.2 3.3 fusion.4
  202.5 15.2 %all-reduce.5.cloned.1.call-done = bf16[1,1024,768]{2,1,0:T(8,128)(2,1)} async-done(((bf16[1,1024,768]{2,1,0:T(8,128)(2,1)}), bf16[1,1024,768]{2,1,0:T(8,128)(2,1)}) %all-reduce.5.cloned.1.call-update) | async-done | bytes 1572880 | tf_op jit(solution)/shard_map/psum | solution.py:113
  217.7 1.8 convert_element_type.118
  219.6 1.2 multiply_reduce_fusion.2
  220.8 2.4 multiply_reduce_fusion.3
  223.2 1.5 collective-permute-start
  224.8 2.1 collective-permute-done
  226.9 1.5 collective-permute-start.1
  228.3 2.1 collective-permute-done.1
  230.4 2.4 collective-permute-start.2
  232.8 1.9 convert_element_type.92
  234.7 11.4 %reduce-scatter.12.cloned.1.call-done = f32[96,192]{1,0:T(8,128)} async-done(((f32[768,192]{1,0:T(8,128)}), f32[96,192]{1,0:T(8,128)}) %reduce-scatter.12.cloned.1.call-update) | async-done | bytes 73744
  246.1 1.6 copy.133
  247.7 0.9 copy.125
  249.2 26.3 %reduce-scatter.10.cloned.1.call-done = bf16[192,1024]{1,0:T(8,128)(2,1)} async-done(((bf16[768,1024]{1,0:T(8,128)(2,1)}), bf16[192,1024]{1,0:T(8,128)(2,1)}) %reduce-scatter.10.cloned.1.call-update) | async-done | bytes 393232
  275.5 1.4 reshape_bitcast_fusion
  276.9 1.1 copy.131
  278.0 1.8 add_convert_fusion.1
  279.8 0.9 copy.124
  280.7 67.9 %reduce-scatter.8.cloned.1.call-done = f32[96,3,192]{2,0,1:T(8,128)} async-done(((f32[768,3,192]{2,0,1:T(8,128)}), f32[96,3,192]{2,0,1:T(8,128)}) %reduce-scatter.8.cloned.1.call-update) | async-done | bytes 221200 | tf_op jit(solution)/shard_map/reduce_scatter | solution.py:126
  348.6 1.6 convert_element_type.120
  (62 shorter events, 4.2 us)
Async XLA Ops:
  8.0 19.7 %copy-start = (bf16[768,3,192]{0,2,1:T(8,128)(2,1)S(1)}, bf16[768,3,192]{0,2,1:T(8,128)(2,1)}, u32[]{:S(2)}) copy-start(bf16[768,3,192]{0,2,1:T(8,128)(2,1)} %param.8) | copy-start | bytes 2654212
  11.6 15.2 %copy-start.1 = (bf16[1,1024,768]{2,1,0:T(8,128)(2,1)S(1)}, bf16[1,1024,768]{2,1,0:T(8,128)(2,1)}, u32[]{:S(2)}) copy-start(bf16[1,1024,768]{2,1,0:T(8,128)(2,1)} %param.6) | copy-start | bytes 4718596
  18.9 32.7 %all-to-all-start.2 = ((bf16[8,2,12288]{2,1,0:T(2,128)(2,1)}), bf16[8,2,12288]{2,1,0:T(2,128)(2,1)S(1)}, u32[]{:S(2)}, u32[]{:S(2)}) async-start(bf16[8,2,12288]{2,1,0:T(2,128)(2,1)} %reshape.160), calls=%async_computation.2 | async-start | bytes 786432 | tf_op jit(solution)/shard_map/all_to_all | solution.py:106
  26.7 0.9 copy-start.15
  51.6 6.3 %copy-start.14 = (s32[8,16,2]{1,2,0:T(2,128)S(1)}, s32[8,16,2]{1,2,0:T(2,128)}, u32[]{:S(2)}) copy-start(s32[8,16,2]{1,2,0:T(2,128)} %param.10) | copy-start | bytes 3076
  51.6 6.6 %copy-start.8 = (bf16[8,2,12288]{2,1,0:T(2,128)(2,1)}, bf16[8,2,12288]{2,1,0:T(2,128)(2,1)S(1)}, u32[]{:S(2)}) copy-start(bf16[8,2,12288]{2,1,0:T(2,128)(2,1)S(1)} %all-to-all-done.2) | copy-start | bytes 1179652
  51.6 34.5 %all-to-all-start = ((bf16[8,2,36864]{2,1,0:T(2,128)(2,1)}), bf16[8,2,36864]{2,1,0:T(2,128)(2,1)}, u32[]{:S(2)}, u32[]{:S(2)}) async-start(bf16[8,2,36864]{2,1,0:T(2,128)(2,1)} %reshape.158), calls=%async_computation | async-start | bytes 2359296 | tf_op jit(solution)/shard_map/all_to_all | solution.py:87
  109.7 1.5 copy-start.2
  109.7 1.5 copy-start.6
  109.7 1.7 copy-start.10
  119.7 2.4 copy-start.3
  119.7 2.4 copy-start.7
  119.7 2.5 copy-start.11
  119.7 2.7 copy-start.12
  119.7 2.8 copy-start.13
  124.4 1.1 copy-start.5
  166.1 14.5 %all-to-all-start.1 = ((bf16[8,128,192]{1,2,0:T(8,128)(2,1)}), bf16[8,128,192]{1,2,0:T(8,128)(2,1)S(1)}, u32[]{:S(2)}, u32[]{:S(2)}) async-start(bf16[8,128,192]{1,2,0:T(8,128)(2,1)} %bitcast.10), calls=%async_computation.1 | async-start | bytes 786432 | tf_op jit(solution)/shard_map/all_to_all | solution.py:93
  169.5 48.2 %all-reduce.5.cloned.1.call-start = ((), (), s32[]{:S(2)}) async-start(), calls=%async_computation.7 | async-start | bytes 3145728 | tf_op jit(solution)/shard_map/psum | solution.py:113
  173.4 10.2 %copy-start.9 = (bf16[192,768]{1,0:T(8,128)(2,1)S(1)}, bf16[192,768]{1,0:T(8,128)(2,1)}, u32[]{:S(2)}) copy-start(bf16[192,768]{1,0:T(8,128)(2,1)} %param.9) | copy-start | bytes 884740
  173.5 72.7 %reduce-scatter.12.cloned.1.call-start = ((), (), s32[]{:S(2)}) async-start(), calls=%async_computation.10 | async-start | bytes 884736
  183.6 91.9 %reduce-scatter.10.cloned.1.call-start = ((), (), s32[]{:S(2)}) async-start(), calls=%async_computation.9 | async-start | bytes 1966080
  197.7 151.0 %reduce-scatter.8.cloned.1.call-start = ((), (), s32[]{:S(2)}) async-start(), calls=%async_computation.8 | async-start | bytes 2654208 | tf_op jit(solution)/shard_map/reduce_scatter | solution.py:126
  217.7 1.9 copy-start.4
  223.2 3.6 %collective-permute-start = (f32[192]{0:T(256)S(1)}, f32[192]{0:T(256)S(1)}, u32[]{:S(2)}, u32[]{:S(2)}) collective-permute-start(f32[192]{0:T(256)S(1)} %get-tuple-element.46), channel_id=1, source_target_pairs={{0,4},{4,0},{8,12},{12,8},{16,20},{20,16},{24,28},{28,24},{1,5},{5... | collective-permute-start | bytes 2312 | tf_op jit(solution)/shard_map/ppermute | solution.py:131
  226.9 3.6 collective-permute-start.1
  230.4 18.2 %collective-permute-start.2 = (f32[192]{0:T(256)S(1)}, f32[192]{0:T(256)S(1)}, u32[]{:S(2)}, u32[]{:S(2)}) collective-permute-start(f32[192]{0:T(256)S(1)} %add.69), channel_id=1, source_target_pairs={{0,16},{4,20},{8,24},{12,28},{16,0},{20,4},{24,8},{28,12},{1,17},{... | collective-permute-start | bytes 2312 | tf_op jit(solution)/shard_map/ppermute | solution.py:131
Sparse Core Ops, SparseCore 0:
  173.6 44.1 all-reduce.4
Sparse Core Ops, SparseCore 1:
  183.7 62.4 reduce-scatter.11
  248.5 26.9 reduce-scatter.9
  278.8 69.7 reduce-scatter.7
